TPU v7x, 32 devices: a whole 2x2x4 slice. The times are simulated.
32 devices in a mesh: dp: 8 (over y, x, core), fsdp: 4 (over z).
Axes of the slice: x: 2, y: 2, z: 4, core: 2. Of those that a mesh axis runs over, the one named last changes fastest.
Arguments:
- glu_frames: bfloat16 [8192, 1536], P(('dp', 'fsdp')), may hold values from -6 to 6
- residual_frames: bfloat16 [8192, 1536], P(('dp', 'fsdp')), may hold values from -6 to 6
- send_rows: int32 [8, 4, 8, 32], P('dp', 'fsdp'), may hold values from 0 to 255, as said below
- recv_slot: int32 [8, 4, 128], P('dp', 'fsdp'), may hold values from 0 to 255, as said below
- segment_ids: int32 [8, 4, 128], P('dp', 'fsdp'), may hold values from 0 to 15, never falling along the last dimension, each value on 1 to 64 neighbouring positions
- code_targets: int32 [8, 512], P('dp'), may hold values from 0 to 8191
- conv_kernel: float32 [31, 1536], replicated, may hold values from -1 to 1
- norm_gain: float32 [1536], replicated, may hold values from 0.5 to 1.5
- point_weight: bfloat16 [1536, 1536], P('fsdp'), may hold values from -0.15625 to 0.15625
- code_head: bfloat16 [1536, 8192], P(None, 'fsdp')
Outputs:
- loss: float32 [], replicated
- grad_head: float32 [1536, 8192], P('dp', 'fsdp')
- grad_point: float32 [1536, 1536], P('fsdp', 'dp')
- grad_kernel: float32 [31, 1536], replicated
- grad_gain: float32 [1536], replicated
- grad_residual: bfloat16 [4096, 1536], P(('dp', 'fsdp'))
- grad_glu: bfloat16 [4096, 1536], P(('dp', 'fsdp'))
Inputs may be any that keep to these rules, and one draw needn't show every extreme that they name: send_rows[i, f, o] lists 32 local slots of loading device (i, f) for owner (o, f). Each loading device fills whole buckets for between 2 and 8 owners, at most one bucket per owner, with distinct slots; its entries for other owners are never read. recv_slot[o, f, r] = i * 32 + c names position c of the bucket from loading device (i, f). Each owner reads 4 full buckets of 32 frames, from distinct loading devices, each whole and in order.
All inputs are finite; a program needn't handle non-finite values.
Results may differ from a plain program's by a relative error of at most 0.012.
The roundings to bfloat16 on the way count: a program that leaves them out, or rounds other values in their place, can miss the bound.
Values may be sent and summed in bfloat16 or wider, within the bound.
No kernel may reach another device: no remote copies, remote signals or barrier semaphores. Data moves between devices by JAX's collectives and lax.ppermute only.
A program may use at most 128 MiB of HBM per device.

v0:
```python
import jax
import jax.numpy as jnp
from jax import lax
from jax.sharding import PartitionSpec as P


def merged(value, axis, join):
    pieces = jax.tree.map(lambda part: lax.all_gather(part, axis), value)
    head = jax.tree.map(lambda part: part[0], pieces)
    tail = jax.tree.map(lambda part: part[1:], pieces)
    subtotal, _ = lax.scan(lambda subtotal, share: (join(subtotal, share), None), head, tail)
    return subtotal


def join_softmax(former, latter):
    joined_top = jnp.maximum(former[0], latter[0])
    joined_sum = former[1] * jnp.exp(former[0] - joined_top) + latter[1] * jnp.exp(
        latter[0] - joined_top
    )
    return (joined_top, joined_sum)


def local(
    glu_frames,
    residual_frames,
    send_rows,
    recv_slot,
    segment_ids,
    code_targets,
    conv_kernel,
    norm_gain,
    point_weight,
    code_head,
):
    feature_width = glu_frames.shape[1]
    tap_count = conv_kernel.shape[0]
    half_taps = tap_count // 2
    slot_list = recv_slot[0, 0]
    row_count = slot_list.shape[0]
    picked_rows = send_rows[0, 0]
    glu_sent = glu_frames[picked_rows]
    residual_sent = residual_frames[picked_rows]
    glu_recv, residual_recv = (
        lax.all_to_all(glu_sent, "dp", split_axis=0, concat_axis=0, tiled=True),
        lax.all_to_all(residual_sent, "dp", split_axis=0, concat_axis=0, tiled=True),
    )
    glu_owned = glu_recv.reshape(-1, feature_width)[slot_list]
    residual_owned = residual_recv.reshape(-1, feature_width)[slot_list]
    segments = segment_ids[0, 0]
    seg_pad = jnp.pad(segments, (half_taps, half_taps), constant_values=-1)
    glu_pad = jnp.pad(glu_owned.astype(jnp.float32), ((half_taps, half_taps), (0, 0)))
    conv_out = jnp.zeros((row_count, feature_width), jnp.float32)
    kept_list = []
    for offset in range(tap_count):
        same_seg = (seg_pad[offset : offset + row_count] == segments)[:, None]
        kept = jnp.where(same_seg, glu_pad[offset : offset + row_count], 0.0)
        kept_list.append(kept)
        conv_out = conv_out + conv_kernel[offset] * kept
    centred = conv_out - jnp.mean(conv_out, axis=1, keepdims=True)
    inv_std = lax.rsqrt(jnp.mean(centred * centred, axis=1, keepdims=True) + 1e-05)
    standard = centred * inv_std
    normed = standard * norm_gain
    gate_sig = jax.nn.sigmoid(normed)
    activation = (normed * gate_sig).astype(jnp.bfloat16)
    full_panel = lax.all_gather(point_weight, "fsdp", axis=0, tiled=True)
    branch_out = jnp.dot(activation, full_panel, preferred_element_type=jnp.float32)
    residual_new = (residual_owned.astype(jnp.float32) + branch_out).astype(jnp.bfloat16)
    group_rows = lax.all_gather(residual_new, "fsdp", axis=0, tiled=True)
    logits = jnp.dot(group_rows, code_head, preferred_element_type=jnp.float32)
    code_local = code_head.shape[1]
    fsdp_index = lax.axis_index("fsdp")
    local_target = code_targets[0] - fsdp_index * code_local
    target_hits = local_target[:, None] == lax.broadcasted_iota(jnp.int32, (1, code_local), 1)
    row_top = jnp.max(logits, axis=1)
    row_sum = jnp.sum(jnp.exp(logits - row_top[:, None]), axis=1)
    pick_total = jnp.sum(jnp.where(target_hits, logits, 0.0))
    merged_top, merged_sum = merged((row_top, row_sum), "fsdp", join_softmax)
    log_norm = merged_top + jnp.log(merged_sum)
    loss_part = (
        jnp.sum(lax.dynamic_slice_in_dim(log_norm, fsdp_index * row_count, row_count, 0))
        - pick_total
    )
    logit_grad = (jnp.exp(logits - log_norm[:, None]) - target_hits.astype(jnp.float32)).astype(
        jnp.bfloat16
    )
    head_local = lax.dot_general(
        group_rows, logit_grad, (((0,), (0,)), ((), ())), preferred_element_type=jnp.float32
    )
    grad_head = lax.psum_scatter(
        head_local.astype(jnp.bfloat16), "dp", scatter_dimension=0, tiled=True
    ).astype(jnp.float32)
    grad_residual = lax.psum_scatter(
        lax.dot_general(
            logit_grad, code_head, (((1,), (1,)), ((), ())), preferred_element_type=jnp.float32
        ),
        "fsdp",
        scatter_dimension=0,
        tiled=True,
    ).astype(jnp.bfloat16)
    whole_grad = lax.dot_general(
        activation, grad_residual, (((0,), (0,)), ((), ())), preferred_element_type=jnp.float32
    )
    column_sum = lax.psum_scatter(
        whole_grad.astype(jnp.bfloat16), "dp", scatter_dimension=1, tiled=True
    )
    grad_point = lax.psum_scatter(column_sum, "fsdp", scatter_dimension=0, tiled=True).astype(
        jnp.float32
    )
    act_grad = lax.dot_general(
        grad_residual, full_panel, (((1,), (1,)), ((), ())), preferred_element_type=jnp.float32
    )
    normed_grad = act_grad * gate_sig * (1.0 + normed * (1.0 - gate_sig))
    gain_grad = jnp.sum(normed_grad * standard, axis=0)
    scaled = normed_grad * norm_gain
    conv_grad = inv_std * (
        scaled
        - jnp.mean(scaled, axis=1, keepdims=True)
        - standard * jnp.mean(scaled * standard, axis=1, keepdims=True)
    )
    kernel_grad = jnp.stack([jnp.sum(conv_grad * kept, axis=0) for kept in kept_list])
    grad_pad = jnp.pad(conv_grad, ((half_taps, half_taps), (0, 0)))
    glu_grad = jnp.zeros((row_count, feature_width), jnp.float32)
    for offset in range(tap_count):
        begin_row = 2 * half_taps - offset
        same_seg = (seg_pad[begin_row : begin_row + row_count] == segments)[:, None]
        glu_grad = glu_grad + conv_kernel[offset] * jnp.where(
            same_seg, grad_pad[begin_row : begin_row + row_count], 0.0
        )
    loss_sum, kernel_sum, gain_sum = lax.psum((loss_part, kernel_grad, gain_grad), ("dp", "fsdp"))
    loss = loss_sum / (row_count * lax.axis_size("dp") * lax.axis_size("fsdp"))
    return (
        loss,
        grad_head,
        grad_point,
        kernel_sum,
        gain_sum,
        grad_residual,
        glu_grad.astype(jnp.bfloat16),
    )


def solution(mesh):
    placed = (
        P(("dp", "fsdp"), None),
        P(("dp", "fsdp"), None),
        P("dp", "fsdp", None, None),
        P("dp", "fsdp", None),
        P("dp", "fsdp", None),
        P("dp", None),
        P(),
        P(),
        P("fsdp", None),
        P(None, "fsdp"),
    )
    return jax.shard_map(
        local,
        mesh=mesh,
        in_specs=placed,
        out_specs=(
            P(),
            P("dp", "fsdp"),
            P("fsdp", "dp"),
            P(),
            P(),
            P(("dp", "fsdp"), None),
            P(("dp", "fsdp"), None),
        ),
        check_vma=False,
    )
```

profile of v0, /device:TPU:10, one launch (start us, length us, event | category | flops | bytes accessed | tf_op | source)
XLA Modules:
  0.0 533.7 jit_solution(17724211208006265354)
XLA Ops:
  7.2 0.7 all-gather.7.cloned.1.call-update
  7.9 0.7 compare_select_fusion
  8.7 2.1 gather_fusion.2
  10.8 4.4 all-to-all-start.1
  15.2 2.1 gather_fusion
  17.7 8.6 %all-to-all-done.1 = bf16[8,32,1536]{2,1,0:T(8,128)(2,1)S(1)} async-done(((bf16[8,32,1536]{2,1,0:T(8,128)(2,1)}), bf16[8,32,1536]{2,1,0:T(8,128)(2,1)S(1)}, u32[]{:S(2)}, u32[]{:S(2)}) %all-to-all-start.1) | async-done | bytes 786464 | tf_op jit(solution)/shard_map/all_to_all | solution.py:44
  26.3 5.0 all-to-all-start
  31.3 0.3 slice_reduce_fusion.30
  31.8 0.7 fusion.124
  32.5 0.7 fusion.123
  33.3 0.9 gather_fusion.3
  34.2 8.2 %all-to-all-done = bf16[8,32,1536]{2,1,0:T(8,128)(2,1)S(1)} async-done(((bf16[8,32,1536]{2,1,0:T(8,128)(2,1)}), bf16[8,32,1536]{2,1,0:T(8,128)(2,1)S(1)}, u32[]{:S(2)}, u32[]{:S(2)}) %all-to-all-start) | async-done | bytes 786464 | tf_op jit(solution)/shard_map/all_to_all | solution.py:45
  42.4 0.9 gather_fusion.1
  43.7 5.2 fusion.155
  49.0 0.2 multiply_reduce_fusion.33
  49.2 48.4 %all-gather.7.cloned.1.call-done = bf16[1536,1536]{1,0:T(8,128)(2,1)} async-done(((bf16[384,1536]{1,0:T(8,128)(2,1)}), bf16[1536,1536]{1,0:T(8,128)(2,1)}) %all-gather.7.cloned.1.call-update) | async-done | bytes 4718608 | tf_op jit(solution)/shard_map/all_gather | solution.py:65
  97.6 4.0 fusion.1
  101.9 37.0 %all-gather.9.cloned.1.call-done = bf16[512,1536]{1,0:T(8,128)(2,1)} async-done(((bf16[128,1536]{1,0:T(8,128)(2,1)}), bf16[512,1536]{1,0:T(8,128)(2,1)}) %all-gather.9.cloned.1.call-update) | async-done | bytes 1572880 | tf_op jit(solution)/shard_map/all_gather | solution.py:68
  138.9 6.1 %fusion.156 = (f32[512]{0:T(512)S(1)}, f32[512,2048]{1,0:T(8,128)S(1)}) fusion(bf16[512,1536]{1,0:T(8,128)(2,1)} %all-gather.9.cloned.1.call-done, bf16[1536,2048]{1,0:T(8,128)(2,1)} %param.21), kind=kOutput, calls=%fused_computation.345 | convolution fusion | flops 3222273536 | bytes 12060672 | tf_op jit(solution)/shard_map/dot_general | solution.py:69
  145.0 2.0 copy-done.2
  147.0 2.9 select_reduce_fusion
  149.9 10.8 %all-gather.3 = f32[4,1,512]{2,1,0:T(1,128)S(1)} all-gather(f32[1,1,512]{2,1,0:T(1,128)S(1)} %bitcast.48), channel_id=3, replica_groups=mesh['dp'=8,'fsdp'=4] {'fsdp'}, dimensions={0}, use_global_device_ids=true | all-gather | bytes 10240 | tf_op jit(solution)/shard_map/all_gather | solution.py:8
  160.8 11.6 %all-gather.2 = f32[4,1,512]{2,1,0:T(1,128)S(1)} all-gather(f32[1,1,512]{2,1,0:T(1,128)S(1)} %bitcast.47), channel_id=2, replica_groups=mesh['dp'=8,'fsdp'=4] {'fsdp'}, dimensions={0}, use_global_device_ids=true | all-gather | bytes 10240 | tf_op jit(solution)/shard_map/all_gather | solution.py:8
  172.5 9.3 %fusion.154 = f32[512,1536]{1,0:T(8,128)} fusion(bf16[1536,2048]{1,0:T(8,128)(2,1)} %param.21, f32[512,2048]{1,0:T(8,128)} %copy-done.2, f32[512]{0:T(512)S(1)} %log_add_fusion, s32[512]{0:T(512)S(1)} %bitcast.50), kind=kOutput, calls=%fused_computation.343 | convolution fusion | flops 3226468352 | bytes 13635584 | tf_op jit(solution)/shard_map/dot_general | solution.py:93
  181.9 60.7 %reduce-scatter.9.cloned.1.call-done = f32[128,1536]{1,0:T(8,128)} async-done(((f32[512,1536]{1,0:T(8,128)}), f32[128,1536]{1,0:T(8,128)}) %reduce-scatter.9.cloned.1.call-update) | async-done | bytes 786448 | tf_op jit(solution)/shard_map/reduce_scatter | solution.py:92
  242.6 1.2 convert_element_type.47
  243.8 3.8 convolution_convert_fusion.1
  247.6 9.1 %convolution_convert_fusion = bf16[1536,2048]{1,0:T(8,128)(2,1)} fusion(bf16[512,1536]{1,0:T(8,128)(2,1)} %all-gather.9.cloned.1.call-done, f32[512,2048]{1,0:T(8,128)} %copy-done.2, f32[512]{0:T(512)S(1)} %log_add_fusion, s32[512]{0:T(512)S(1)} %bitcast.51), kind=kOutput, calls=%fused_computation.7 | convolution fusion | flops 3229614080 | bytes 12062720 | tf_op jit(solution)/shard_map/dot_general | solution.py:86
  256.8 0.3 reduce-scatter.13.cloned.1.call-start
  257.0 0.7 dynamic-slice_reduce_fusion
  259.1 6.1 %multiply_reduce_fusion = (f32[1536]{0:T(1024)}, f32[128]{0:T(128)S(1)}, f32[128]{0:T(128)S(1)}, f32[128,1536]{1,0:T(8,128)}) fusion(f32[128,1536]{1,0:T(8,128)S(1)} %get-tuple-element.120, f32[128]{0:T(128)S(1)} %add_rsqrt_fusion, f32[128]{0:T(128)S(1)} %broadcast_multiply_fusion.2, f32[1536]{0:T(1024)S(1)} %copy-done.5, ...), kind=kOutput, calls=%fused_computation.198 | convolution fusion | flops 607320320 | bytes 6699008 | tf_op jit(solution)/shard_map/dot_general | solution.py:109
  265.1 0.5 broadcast_multiply_fusion
  265.7 36.4 %reduce-scatter.11.cloned.1.call-done = bf16[1536,192]{0,1:T(8,128)(2,1)} async-done(((bf16[1536,1536]{0,1:T(8,128)(2,1)}), bf16[1536,192]{0,1:T(8,128)(2,1)}) %reduce-scatter.11.cloned.1.call-update) | async-done | bytes 589840 | tf_op jit(solution)/shard_map/reduce_scatter | solution.py:103
  302.1 2.2 copy.17
  304.4 3.0 multiply_reduce_fusion.1
  307.8 1.2 multiply_reduce_fusion.29
  309.3 2.3 multiply_reduce_fusion.20
  311.6 2.3 multiply_reduce_fusion.10
  314.2 2.8 stack.127
  317.3 6.3 %fusion.108 = bf16[128,1536]{1,0:T(8,128)(2,1)} fusion(f32[128,1536]{1,0:T(8,128)S(1)} %get-tuple-element.118, f32[1536]{0:T(1024)S(1)} %copy-done.63, f32[1536]{0:T(1024)S(1)} %copy-done.65, f32[1536]{0:T(1024)S(1)} %copy-done.7, f32[1536]{0:T(1024)S(1)} %copy-done.9, f32[1536]{0:T(1024)S(1)} %copy-done.11, f32[1536]{0:T(1024)S(1)} %copy-done.13, ...), kind=kLoop, calls=%fused_computation.183 | loop fusion | flops 18087936 | bytes 1373952 | tf_op jit(solution)/shard_map/convert_element_type | solution.py:138
  323.6 40.7 %all-reduce.3 = (f32[]{:T(128)}, f32[1536]{0:T(1024)}) all-reduce(f32[]{:T(128)S(6)} %sub.70, f32[1536]{0:T(1024)S(1)} %copy-done.85), channel_id=1, replica_groups=mesh['dp'=8,'fsdp'=4] {'dp','fsdp'}, use_global_device_ids=true, to_apply=%region_8.9 | all-reduce | flops 1537 | bytes 12296 | tf_op jit(solution)/shard_map/psum | solution.py:129
  365.0 3.3 reduce-scatter.7.cloned.1.call-done
  368.3 2.5 convert_element_type.46
  370.8 21.2 %reduce-scatter.13.cloned.1.call-done = bf16[384,192]{1,0:T(8,128)(2,1)} async-done(((bf16[1536,192]{1,0:T(8,128)(2,1)}), bf16[384,192]{1,0:T(8,128)(2,1)}) %reduce-scatter.13.cloned.1.call-update) | async-done | bytes 147472
  392.0 1.1 copy.18
  393.1 0.7 convert_element_type.49
  393.8 130.3 %all-reduce.6.cloned.1.call-done = f32[31,1536]{1,0:T(8,128)} async-done(((f32[31,1536]{1,0:T(8,128)}), f32[31,1536]{1,0:T(8,128)}) %all-reduce.6.cloned.1.call-update) | async-done | bytes 190480 | tf_op jit(solution)/shard_map/psum | solution.py:129
  524.1 1.6 copy.35
  (245 shorter events, 1.7 us)
Async XLA Ops:
  7.2 90.5 %all-gather.7.cloned.1.call-start = ((), (), s32[]{:S(2)}) async-start(), calls=%async_computation.6 | async-start | bytes 5898240 | tf_op jit(solution)/shard_map/all_gather | solution.py:65
  10.8 15.5 %all-to-all-start.1 = ((bf16[8,32,1536]{2,1,0:T(8,128)(2,1)}), bf16[8,32,1536]{2,1,0:T(8,128)(2,1)S(1)}, u32[]{:S(2)}, u32[]{:S(2)}) async-start(bf16[8,32,1536]{2,1,0:T(8,128)(2,1)} %bitcast.8), calls=%async_computation.1 | async-start | bytes 1572864 | tf_op jit(solution)/shard_map/all_to_all | solution.py:44
  15.2 16.6 %copy-start.88 = (s32[1,1,128]{2,1,0:T(1,128)S(1)}, s32[1,1,128]{2,1,0:T(1,128)}, u32[]{:S(2)}) copy-start(s32[1,1,128]{2,1,0:T(1,128)} %param.16) | copy-start | bytes 1540
  17.6 25.8 %copy-start.42 = (f32[1536]{0:T(1024)}, f32[1536]{0:T(1024)S(1)}, u32[]{:S(2)}) copy-start(f32[1536]{0:T(1024)S(1)} %get-tuple-element.92) | copy-start | bytes 18436
  17.6 25.8 %copy-start.44 = (f32[1536]{0:T(1024)}, f32[1536]{0:T(1024)S(1)}, u32[]{:S(2)}) copy-start(f32[1536]{0:T(1024)S(1)} %get-tuple-element.93) | copy-start | bytes 18436
  17.6 25.8 %copy-start.46 = (f32[1536]{0:T(1024)}, f32[1536]{0:T(1024)S(1)}, u32[]{:S(2)}) copy-start(f32[1536]{0:T(1024)S(1)} %get-tuple-element.94) | copy-start | bytes 18436
  17.6 25.8 %copy-start.48 = (f32[1536]{0:T(1024)}, f32[1536]{0:T(1024)S(1)}, u32[]{:S(2)}) copy-start(f32[1536]{0:T(1024)S(1)} %get-tuple-element.95) | copy-start | bytes 18436
  17.6 25.8 %copy-start.50 = (f32[1536]{0:T(1024)}, f32[1536]{0:T(1024)S(1)}, u32[]{:S(2)}) copy-start(f32[1536]{0:T(1024)S(1)} %get-tuple-element.96) | copy-start | bytes 18436
  17.6 25.8 %copy-start.52 = (f32[1536]{0:T(1024)}, f32[1536]{0:T(1024)S(1)}, u32[]{:S(2)}) copy-start(f32[1536]{0:T(1024)S(1)} %get-tuple-element.97) | copy-start | bytes 18436
  17.7 25.8 %copy-start.54 = (f32[1536]{0:T(1024)}, f32[1536]{0:T(1024)S(1)}, u32[]{:S(2)}) copy-start(f32[1536]{0:T(1024)S(1)} %get-tuple-element.98) | copy-start | bytes 18436
  17.7 25.8 %copy-start.56 = (f32[1536]{0:T(1024)}, f32[1536]{0:T(1024)S(1)}, u32[]{:S(2)}) copy-start(f32[1536]{0:T(1024)S(1)} %get-tuple-element.99) | copy-start | bytes 18436
  17.7 25.8 %copy-start.58 = (f32[1536]{0:T(1024)}, f32[1536]{0:T(1024)S(1)}, u32[]{:S(2)}) copy-start(f32[1536]{0:T(1024)S(1)} %get-tuple-element.100) | copy-start | bytes 18436
  17.7 25.8 %copy-start.60 = (f32[1536]{0:T(1024)}, f32[1536]{0:T(1024)S(1)}, u32[]{:S(2)}) copy-start(f32[1536]{0:T(1024)S(1)} %get-tuple-element.101) | copy-start | bytes 18436
  17.7 25.8 %copy-start.62 = (f32[1536]{0:T(1024)}, f32[1536]{0:T(1024)S(1)}, u32[]{:S(2)}) copy-start(f32[1536]{0:T(1024)S(1)} %get-tuple-element.102) | copy-start | bytes 18436
  17.7 25.8 %copy-start.64 = (f32[1536]{0:T(1024)}, f32[1536]{0:T(1024)S(1)}, u32[]{:S(2)}) copy-start(f32[1536]{0:T(1024)S(1)} %get-tuple-element.103) | copy-start | bytes 18436
  26.3 16.1 %all-to-all-start = ((bf16[8,32,1536]{2,1,0:T(8,128)(2,1)}), bf16[8,32,1536]{2,1,0:T(8,128)(2,1)S(1)}, u32[]{:S(2)}, u32[]{:S(2)}) async-start(bf16[8,32,1536]{2,1,0:T(8,128)(2,1)} %bitcast.3), calls=%async_computation | async-start | bytes 1572864 | tf_op jit(solution)/shard_map/all_to_all | solution.py:45
  31.3 107.6 %all-gather.9.cloned.1.call-start = ((), (), s32[]{:S(2)}) async-start(), calls=%async_computation.7 | async-start | bytes 1966080 | tf_op jit(solution)/shard_map/all_gather | solution.py:68
  31.6 11.9 %copy-start.6 = (f32[1536]{0:T(1024)}, f32[1536]{0:T(1024)S(1)}, u32[]{:S(2)}) copy-start(f32[1536]{0:T(1024)S(1)} %get-tuple-element.74) | copy-start | bytes 18436
  31.6 11.9 %copy-start.8 = (f32[1536]{0:T(1024)}, f32[1536]{0:T(1024)S(1)}, u32[]{:S(2)}) copy-start(f32[1536]{0:T(1024)S(1)} %get-tuple-element.75) | copy-start | bytes 18436
  31.6 11.9 %copy-start.10 = (f32[1536]{0:T(1024)}, f32[1536]{0:T(1024)S(1)}, u32[]{:S(2)}) copy-start(f32[1536]{0:T(1024)S(1)} %get-tuple-element.76) | copy-start | bytes 18436
  31.7 11.9 %copy-start.12 = (f32[1536]{0:T(1024)}, f32[1536]{0:T(1024)S(1)}, u32[]{:S(2)}) copy-start(f32[1536]{0:T(1024)S(1)} %get-tuple-element.77) | copy-start | bytes 18436
  31.7 11.9 %copy-start.14 = (f32[1536]{0:T(1024)}, f32[1536]{0:T(1024)S(1)}, u32[]{:S(2)}) copy-start(f32[1536]{0:T(1024)S(1)} %get-tuple-element.78) | copy-start | bytes 18436
  31.7 11.9 %copy-start.16 = (f32[1536]{0:T(1024)}, f32[1536]{0:T(1024)S(1)}, u32[]{:S(2)}) copy-start(f32[1536]{0:T(1024)S(1)} %get-tuple-element.79) | copy-start | bytes 18436
  31.7 11.9 %copy-start.18 = (f32[1536]{0:T(1024)}, f32[1536]{0:T(1024)S(1)}, u32[]{:S(2)}) copy-start(f32[1536]{0:T(1024)S(1)} %get-tuple-element.80) | copy-start | bytes 18436
  31.7 11.9 %copy-start.20 = (f32[1536]{0:T(1024)}, f32[1536]{0:T(1024)S(1)}, u32[]{:S(2)}) copy-start(f32[1536]{0:T(1024)S(1)} %get-tuple-element.81) | copy-start | bytes 18436
  31.7 11.9 %copy-start.22 = (f32[1536]{0:T(1024)}, f32[1536]{0:T(1024)S(1)}, u32[]{:S(2)}) copy-start(f32[1536]{0:T(1024)S(1)} %get-tuple-element.82) | copy-start | bytes 18436
  31.7 11.9 %copy-start.24 = (f32[1536]{0:T(1024)}, f32[1536]{0:T(1024)S(1)}, u32[]{:S(2)}) copy-start(f32[1536]{0:T(1024)S(1)} %get-tuple-element.83) | copy-start | bytes 18436
  31.7 11.9 %copy-start.26 = (f32[1536]{0:T(1024)}, f32[1536]{0:T(1024)S(1)}, u32[]{:S(2)}) copy-start(f32[1536]{0:T(1024)S(1)} %get-tuple-element.84) | copy-start | bytes 18436
  33.2 15.6 %copy-start.66 = (pred[128]{0:T(512)(128)(4,1)}, pred[128]{0:T(512)(128)(4,1)S(1)}, u32[]{:S(2)}) copy-start(pred[128]{0:T(512)(128)(4,1)S(1)} %get-tuple-element.124) | copy-start | bytes 388
  33.2 15.7 %copy-start.68 = (pred[128]{0:T(512)(128)(4,1)}, pred[128]{0:T(512)(128)(4,1)S(1)}, u32[]{:S(2)}) copy-start(pred[128]{0:T(512)(128)(4,1)S(1)} %get-tuple-element.125) | copy-start | bytes 388
  33.2 15.7 %copy-start.70 = (pred[128]{0:T(512)(128)(4,1)}, pred[128]{0:T(512)(128)(4,1)S(1)}, u32[]{:S(2)}) copy-start(pred[128]{0:T(512)(128)(4,1)S(1)} %get-tuple-element.126) | copy-start | bytes 388
  33.3 15.7 %copy-start.72 = (pred[128]{0:T(512)(128)(4,1)}, pred[128]{0:T(512)(128)(4,1)S(1)}, u32[]{:S(2)}) copy-start(pred[128]{0:T(512)(128)(4,1)S(1)} %get-tuple-element.127) | copy-start | bytes 388
  33.3 15.7 %copy-start.74 = (pred[128]{0:T(512)(128)(4,1)}, pred[128]{0:T(512)(128)(4,1)S(1)}, u32[]{:S(2)}) copy-start(pred[128]{0:T(512)(128)(4,1)S(1)} %get-tuple-element.128) | copy-start | bytes 388
  33.3 15.7 %copy-start.76 = (pred[128]{0:T(512)(128)(4,1)}, pred[128]{0:T(512)(128)(4,1)S(1)}, u32[]{:S(2)}) copy-start(pred[128]{0:T(512)(128)(4,1)S(1)} %get-tuple-element.129) | copy-start | bytes 388
  33.3 15.7 %copy-start.78 = (pred[128]{0:T(512)(128)(4,1)}, pred[128]{0:T(512)(128)(4,1)S(1)}, u32[]{:S(2)}) copy-start(pred[128]{0:T(512)(128)(4,1)S(1)} %get-tuple-element.130) | copy-start | bytes 388
  33.3 15.7 %copy-start.80 = (pred[128]{0:T(512)(128)(4,1)}, pred[128]{0:T(512)(128)(4,1)S(1)}, u32[]{:S(2)}) copy-start(pred[128]{0:T(512)(128)(4,1)S(1)} %get-tuple-element.131) | copy-start | bytes 388
  33.3 15.7 %copy-start.82 = (pred[128]{0:T(512)(128)(4,1)}, pred[128]{0:T(512)(128)(4,1)S(1)}, u32[]{:S(2)}) copy-start(pred[128]{0:T(512)(128)(4,1)S(1)} %get-tuple-element.132) | copy-start | bytes 388
  34.2 63.4 %copy-start.5 = (f32[1536]{0:T(1024)S(1)}, f32[1536]{0:T(1024)}, u32[]{:S(2)}) copy-start(f32[1536]{0:T(1024)} %param.19) | copy-start | bytes 18436
  49.0 210.1 %copy-start.84 = (f32[128]{0:T(128)}, f32[128]{0:T(128)S(1)}, u32[]{:S(2)}) copy-start(f32[128]{0:T(128)S(1)} %broadcast_multiply_fusion.2) | copy-start | bytes 1540
  49.2 209.8 %copy-start.86 = (f32[128]{0:T(128)}, f32[128]{0:T(128)S(1)}, u32[]{:S(2)}) copy-start(f32[128]{0:T(128)S(1)} %add_rsqrt_fusion) | copy-start | bytes 1540
  49.2 52.7 %copy-start.87 = (s32[1,512]{1,0:T(1,128)S(1)}, s32[1,512]{1,0:T(1,128)}, u32[]{:S(2)}) copy-start(s32[1,512]{1,0:T(1,128)} %param.17) | copy-start | bytes 6148
  101.7 140.9 %reduce-scatter.9.cloned.1.call-start = ((), (), s32[]{:S(2)}) async-start(), calls=%async_computation.9 | async-start | bytes 3932160 | tf_op jit(solution)/shard_map/reduce_scatter | solution.py:92
  181.8 120.2 %reduce-scatter.11.cloned.1.call-start = ((), (), s32[]{:S(2)}) async-start(), calls=%async_computation.10 | async-start | bytes 5308416 | tf_op jit(solution)/shard_map/reduce_scatter | solution.py:103
  243.8 15.3 %copy-start.3 = (bf16[128,1536]{1,0:T(8,128)(2,1)}, bf16[128,1536]{1,0:T(8,128)(2,1)S(1)}, u32[]{:S(2)}) copy-start(bf16[128,1536]{1,0:T(8,128)(2,1)S(1)} %convert_element_type.47) | copy-start | bytes 1179652
  247.6 120.7 %reduce-scatter.7.cloned.1.call-start = ((), (), s32[]{:S(2)}) async-start(), calls=%async_computation.8 | async-start | bytes 7077888 | tf_op jit(solution)/shard_map/reduce_scatter | solution.py:89
  256.8 135.2 %reduce-scatter.13.cloned.1.call-start = ((), (), s32[]{:S(2)}) async-start(), calls=%async_computation.12 | async-start | bytes 983040
  304.3 219.8 %all-reduce.6.cloned.1.call-start = ((), (), s32[]{:S(2)}) async-start(), calls=%async_computation.11 | async-start | bytes 393216 | tf_op jit(solution)/shard_map/psum | solution.py:129
  307.8 15.8 %copy-start.85 = (f32[1536]{0:T(1024)S(1)}, f32[1536]{0:T(1024)}, u32[]{:S(2)}) copy-start(f32[1536]{0:T(1024)} %get-tuple-element.39) | copy-start | bytes 18436
  (51 other events, 477.5 us)
Sparse Core Ops, SparseCore 0:
  9.6 88.0 all-gather.6
  101.8 37.0 all-gather.8
  182.0 60.5 reduce-scatter.8
  247.7 54.3 reduce-scatter.10
  305.7 62.5 reduce-scatter.6
  370.5 21.4 reduce-scatter.12
  398.1 125.9 all-reduce.5
where the time goes:
time: 534 us
  waiting for transfers between devices  355 us (66%)
  blocking collectives  63.2 us (12%)
  matrix products  38.3 us (7%)
  other arithmetic  31.3 us (6%)
  between operations  19 us (4%)
  local copies, waits for them, and re-layouts  16.9 us (3%)
  starting transfers between devices  10 us (2%)
    psum x1, waiting for transfers between devices, local(): lax.psum((loss_part, kernel_grad, gain_grad), ('dp', 'fsdp'))  130 us
    reduce_scatter x1, waiting for transfers between devices, local(): lax.psum_scatter(lax.dot_general(logit_grad, code_head, (((1,), (1,)), ((...  60.7 us
    all_gather x1, waiting for transfers between devices, local(): full_panel = lax.all_gather(point_weight, 'fsdp', axis=0, tiled=True)  48.4 us
    psum x1, blocking collectives, local(): lax.psum((loss_part, kernel_grad, gain_grad), ('dp', 'fsdp'))  40.7 us
    all_gather x1, waiting for transfers between devices, local(): group_rows = lax.all_gather(residual_new, 'fsdp', axis=0, tiled=True)  37 us
    reduce_scatter x1, waiting for transfers between devices, local(): lax.psum_scatter(whole_grad.astype(jnp.bfloat16), 'dp', scatter_dimension...  36.4 us
    all_gather x2, blocking collectives, merged(): pieces = jax.tree.map(lambda part: lax.all_gather(part, axis), value)  22.4 us
    unnamed x8, waiting for transfers between devices  22 us
  transfers between devices with their start and end apart: 9, of which 9 were waited for; matrix products, arithmetic and copies ran while one was open for 10% of the time, Pallas kernels for 0%

commit v1 on v0

--- a/solution.py
+++ b/solution.py
@@ -126,7 +126,9 @@
         glu_grad = glu_grad + conv_kernel[offset] * jnp.where(
             same_seg, grad_pad[begin_row : begin_row + row_count], 0.0
         )
-    loss_sum, kernel_sum, gain_sum = lax.psum((loss_part, kernel_grad, gain_grad), ("dp", "fsdp"))
+    loss_sum, kernel_sum, gain_sum = lax.psum(
+        lax.psum((loss_part, kernel_grad, gain_grad), "fsdp"), "dp"
+    )
     loss = loss_sum / (row_count * lax.axis_size("dp") * lax.axis_size("fsdp"))
     return (
         loss,

time: 534 us -> 498 us (0.933)
  blocking collectives: 63.2 us -> 43.5 us
  waiting for transfers between devices: 355 us -> 338 us
    psum x1 -> x2, waiting for transfers between devices: 130 us -> 88.5 us  [the longest x1 55.4 us: local(): lax.psum(lax.psum((loss_part, kernel_grad, gain_grad), 'fsdp'), 'dp')]
    reduce_scatter x1, waiting for transfers between devices: 3.31 us -> 36.4 us  [local(): lax.psum_scatter(head_local.astype(jnp.bfloat16), 'dp', scatter_dimension...]
    psum x1 -> x2, blocking collectives: 40.7 us -> 21.1 us  [the longest x1 11.2 us: local(): lax.psum(lax.psum((loss_part, kernel_grad, gain_grad), 'fsdp'), 'dp')]
    reduce_scatter x1, waiting for transfers between devices: 36.4 us -> 29.2 us  [local(): lax.psum_scatter(whole_grad.astype(jnp.bfloat16), 'dp', scatter_dimension...]
    unnamed x8 -> x9, waiting for transfers between devices: 22 us -> 22.3 us
  transfers between devices with their start and end apart: 9 -> 10, of which waited for: 9 -> 10; matrix products, arithmetic and copies ran while one was open for 10% -> 11% of each run, Pallas kernels for 0% -> 0%
where the time goes in v1:
time: 498 us; the launch traced here: 495 us
  waiting for transfers between devices  338 us (68%)
  blocking collectives  43.5 us (9%)
  matrix products  37.3 us (7%)
  other arithmetic  28.7 us (6%)
  local copies, waits for them, and re-layouts  18.9 us (4%)
  between operations  18.8 us (4%)
  starting transfers between devices  10.3 us (2%)
    reduce_scatter x1, waiting for transfers between devices, local(): lax.psum_scatter(lax.dot_general(logit_grad, code_head, (((1,), (1,)), ((...  60.7 us
    psum x1, waiting for transfers between devices, local(): lax.psum(lax.psum((loss_part, kernel_grad, gain_grad), 'fsdp'), 'dp')  55.4 us
    all_gather x1, waiting for transfers between devices, local(): full_panel = lax.all_gather(point_weight, 'fsdp', axis=0, tiled=True)  47.9 us
    all_gather x1, waiting for transfers between devices, local(): group_rows = lax.all_gather(residual_new, 'fsdp', axis=0, tiled=True)  36.9 us
    reduce_scatter x1, waiting for transfers between devices, local(): lax.psum_scatter(head_local.astype(jnp.bfloat16), 'dp', scatter_dimension...  36.4 us
    psum x1, waiting for transfers between devices, local(): lax.psum((loss_part, kernel_grad, gain_grad), 'fsdp')  33.1 us
    reduce_scatter x1, waiting for transfers between devices, local(): lax.psum_scatter(whole_grad.astype(jnp.bfloat16), 'dp', scatter_dimension...  29.2 us
    all_gather x2, blocking collectives, merged(): pieces = jax.tree.map(lambda part: lax.all_gather(part, axis), value)  22.4 us
  transfers between devices with their start and end apart: 10, of which 10 were waited for; matrix products, arithmetic and copies ran while one was open for 11% of the time, Pallas kernels for 0%

profile of v1, /device:TPU:10, one launch (start us, length us, event | category | flops | bytes accessed | tf_op | source)
XLA Modules:
  0.0 495.4 jit_solution(9351686138867939087)
XLA Ops:
  7.2 0.7 all-gather.7.cloned.1.call-update
  7.9 0.7 compare_select_fusion
  8.7 2.2 gather_fusion.2
  10.9 4.4 all-to-all-start.1
  15.3 2.1 gather_fusion
  17.4 0.8 slice_reduce_fusion.29
  18.2 8.2 %all-to-all-done.1 = bf16[8,32,1536]{2,1,0:T(8,128)(2,1)S(1)} async-done(((bf16[8,32,1536]{2,1,0:T(8,128)(2,1)}), bf16[8,32,1536]{2,1,0:T(8,128)(2,1)S(1)}, u32[]{:S(2)}, u32[]{:S(2)}) %all-to-all-start.1) | async-done | bytes 786464 | tf_op jit(solution)/shard_map/all_to_all | solution.py:44
  26.3 5.0 %all-to-all-start = ((bf16[8,32,1536]{2,1,0:T(8,128)(2,1)}), bf16[8,32,1536]{2,1,0:T(8,128)(2,1)S(1)}, u32[]{:S(2)}, u32[]{:S(2)}) async-start(bf16[8,32,1536]{2,1,0:T(8,128)(2,1)} %bitcast.3), calls=%async_computation | async-start | bytes 1572864 | tf_op jit(solution)/shard_map/all_to_all | solution.py:45
  31.3 0.9 slice_reduce_fusion.30
  32.2 0.7 fusion.124
  32.9 0.7 fusion.123
  33.7 0.9 gather_fusion.3
  34.6 7.8 %all-to-all-done = bf16[8,32,1536]{2,1,0:T(8,128)(2,1)S(1)} async-done(((bf16[8,32,1536]{2,1,0:T(8,128)(2,1)}), bf16[8,32,1536]{2,1,0:T(8,128)(2,1)S(1)}, u32[]{:S(2)}, u32[]{:S(2)}) %all-to-all-start) | async-done | bytes 786464 | tf_op jit(solution)/shard_map/all_to_all | solution.py:45
  42.4 1.6 gather_fusion.1
  44.1 5.3 %fusion.155 = (f32[128]{0:T(128)S(1)}, f32[128,1536]{1,0:T(8,128)S(1)}) fusion(pred[128]{0:T(512)(128)(4,1)} %get-tuple-element.154, f32[1536]{0:T(1024)} %get-tuple-element.102, pred[128]{0:T(512)(128)(4,1)} %get-tuple-element.126, f32[1536]{0:T(1024)} %get-tuple-element.103, pred[128]{0:T(512)(128)(4,1)} %get-tuple-element.127, ...), kind=kLoop, calls=%fused_computation.344 | loop fusion | flops 18087808 | bytes 1767680 | tf_op jit(solution)/shard_map/reduce_sum | solution.py:59
  49.8 47.9 %all-gather.7.cloned.1.call-done = bf16[1536,1536]{1,0:T(8,128)(2,1)} async-done(((bf16[384,1536]{1,0:T(8,128)(2,1)}), bf16[1536,1536]{1,0:T(8,128)(2,1)}) %all-gather.7.cloned.1.call-update) | async-done | bytes 4718608 | tf_op jit(solution)/shard_map/all_gather | solution.py:65
  97.6 4.1 fusion.1
  102.0 36.9 %all-gather.9.cloned.1.call-done = bf16[512,1536]{1,0:T(8,128)(2,1)} async-done(((bf16[128,1536]{1,0:T(8,128)(2,1)}), bf16[512,1536]{1,0:T(8,128)(2,1)}) %all-gather.9.cloned.1.call-update) | async-done | bytes 1572880 | tf_op jit(solution)/shard_map/all_gather | solution.py:68
  138.9 6.1 %fusion.156 = (f32[512]{0:T(512)S(1)}, f32[512,2048]{1,0:T(8,128)S(1)}) fusion(bf16[512,1536]{1,0:T(8,128)(2,1)} %all-gather.9.cloned.1.call-done, bf16[1536,2048]{1,0:T(8,128)(2,1)} %param.21), kind=kOutput, calls=%fused_computation.345 | convolution fusion | flops 3222273536 | bytes 12060672 | tf_op jit(solution)/shard_map/dot_general | solution.py:69
  145.1 2.0 copy-done.2
  147.1 3.0 select_reduce_fusion
  150.1 10.8 %all-gather.3 = f32[4,1,512]{2,1,0:T(1,128)S(1)} all-gather(f32[1,1,512]{2,1,0:T(1,128)S(1)} %bitcast.48), channel_id=3, replica_groups=mesh['dp'=8,'fsdp'=4] {'fsdp'}, dimensions={0}, use_global_device_ids=true | all-gather | bytes 10240 | tf_op jit(solution)/shard_map/all_gather | solution.py:8
  161.0 11.6 %all-gather.2 = f32[4,1,512]{2,1,0:T(1,128)S(1)} all-gather(f32[1,1,512]{2,1,0:T(1,128)S(1)} %bitcast.47), channel_id=2, replica_groups=mesh['dp'=8,'fsdp'=4] {'fsdp'}, dimensions={0}, use_global_device_ids=true | all-gather | bytes 10240 | tf_op jit(solution)/shard_map/all_gather | solution.py:8
  172.8 9.2 %fusion.154 = f32[512,1536]{1,0:T(8,128)} fusion(bf16[1536,2048]{1,0:T(8,128)(2,1)} %param.21, f32[512,2048]{1,0:T(8,128)} %copy-done.2, f32[512]{0:T(512)S(1)} %log_add_fusion, s32[512]{0:T(512)S(1)} %bitcast.50), kind=kOutput, calls=%fused_computation.343 | convolution fusion | flops 3226468352 | bytes 13635584 | tf_op jit(solution)/shard_map/dot_general | solution.py:93
  182.1 60.7 %reduce-scatter.9.cloned.1.call-done = f32[128,1536]{1,0:T(8,128)} async-done(((f32[512,1536]{1,0:T(8,128)}), f32[128,1536]{1,0:T(8,128)}) %reduce-scatter.9.cloned.1.call-update) | async-done | bytes 786448 | tf_op jit(solution)/shard_map/reduce_scatter | solution.py:92
  242.7 1.2 convert_element_type.47
  243.9 3.8 convolution_convert_fusion.1
  248.2 4.8 multiply_reduce_fusion
  253.2 2.6 multiply_reduce_fusion.1
  255.8 0.6 multiply_reduce_fusion.29
  256.7 1.7 multiply_reduce_fusion.20
  258.5 1.8 multiply_reduce_fusion.10
  260.5 2.8 stack.127
  263.4 9.3 %convolution_convert_fusion = bf16[1536,2048]{1,0:T(8,128)(2,1)} fusion(bf16[512,1536]{1,0:T(8,128)(2,1)} %all-gather.9.cloned.1.call-done, f32[512,2048]{1,0:T(8,128)} %copy-done.2, f32[512]{0:T(512)S(1)} %copy-done.81, s32[512]{0:T(512)S(1)} %bitcast.51), kind=kOutput, calls=%fused_computation.7 | convolution fusion | flops 3229614080 | bytes 12062720 | tf_op jit(solution)/shard_map/dot_general | solution.py:86
  273.1 29.2 %reduce-scatter.11.cloned.1.call-done = bf16[1536,192]{0,1:T(8,128)(2,1)} async-done(((bf16[1536,1536]{0,1:T(8,128)(2,1)}), bf16[1536,192]{0,1:T(8,128)(2,1)}) %reduce-scatter.11.cloned.1.call-update) | async-done | bytes 589840 | tf_op jit(solution)/shard_map/reduce_scatter | solution.py:103
  302.3 2.2 copy.17
  304.8 0.7 dynamic-slice_reduce_fusion
  306.9 33.1 %all-reduce.8.cloned.1.call-done = f32[31,1536]{1,0:T(8,128)} async-done(((f32[31,1536]{1,0:T(8,128)}), f32[31,1536]{1,0:T(8,128)}) %all-reduce.8.cloned.1.call-update) | async-done | bytes 190480 | tf_op jit(solution)/shard_map/psum | solution.py:130
  340.3 6.2 %fusion.108 = bf16[128,1536]{1,0:T(8,128)(2,1)} fusion(f32[128,1536]{1,0:T(8,128)S(1)} %get-tuple-element.120, f32[1536]{0:T(1024)S(1)} %copy-done.34, f32[1536]{0:T(1024)S(1)} %copy-done.35, f32[1536]{0:T(1024)S(1)} %copy-done.6, f32[1536]{0:T(1024)S(1)} %copy-done.7, f32[1536]{0:T(1024)S(1)} %copy-done.8, f32[1536]{0:T(1024)S(1)} %copy-done.9, ...), kind=kLoop, calls=%fused_computation.183 | loop fusion | flops 18087936 | bytes 1373952 | tf_op jit(solution)/shard_map/convert_element_type | solution.py:140
  346.5 9.9 %all-reduce.4 = (f32[]{:T(128)}, f32[1536]{0:T(1024)S(1)}) all-reduce(f32[]{:T(128)S(6)} %sub.70, f32[1536]{0:T(1024)} %get-tuple-element.39), channel_id=1, replica_groups=mesh['dp'=8,'fsdp'=4] {'fsdp'}, use_global_device_ids=true, to_apply=%region_8.9 | all-reduce | flops 1537 | bytes 12296 | tf_op jit(solution)/shard_map/psum | solution.py:130
  356.4 11.2 %all-reduce.3 = (f32[]{:T(128)}, f32[1536]{0:T(1024)}) all-reduce(f32[]{:T(128)} %get-tuple-element.116, f32[1536]{0:T(1024)S(1)} %get-tuple-element.117), channel_id=1, replica_groups=mesh['dp'=8,'fsdp'=4] {'dp'}, use_global_device_ids=true, to_apply=%region_9.10 | all-reduce | flops 1537 | bytes 12296 | tf_op jit(solution)/shard_map/psum | solution.py:129
  368.3 36.4 %reduce-scatter.7.cloned.1.call-done = bf16[192,2048]{1,0:T(8,128)(2,1)} async-done(((bf16[1536,2048]{1,0:T(8,128)(2,1)}), bf16[192,2048]{1,0:T(8,128)(2,1)}) %reduce-scatter.7.cloned.1.call-update) | async-done | bytes 786448 | tf_op jit(solution)/shard_map/reduce_scatter | solution.py:89
  404.7 2.5 convert_element_type.46
  407.1 21.5 %reduce-scatter.13.cloned.1.call-done = bf16[384,192]{1,0:T(8,128)(2,1)} async-done(((bf16[1536,192]{1,0:T(8,128)(2,1)}), bf16[384,192]{1,0:T(8,128)(2,1)}) %reduce-scatter.13.cloned.1.call-update) | async-done | bytes 147472
  428.6 1.1 copy.18
  429.7 0.7 convert_element_type.49
  430.4 55.4 %all-reduce.10.cloned.1.call-done = f32[31,1536]{1,0:T(8,128)} async-done(((f32[31,1536]{1,0:T(8,128)}), f32[31,1536]{1,0:T(8,128)}) %all-reduce.10.cloned.1.call-update) | async-done | bytes 190480 | tf_op jit(solution)/shard_map/psum | solution.py:129
  485.9 1.6 copy.36
  (239 shorter events, 2.3 us)
Async XLA Ops:
  7.2 90.5 %all-gather.7.cloned.1.call-start = ((), (), s32[]{:S(2)}) async-start(), calls=%async_computation.6 | async-start | bytes 5898240 | tf_op jit(solution)/shard_map/all_gather | solution.py:65
  10.9 15.5 %all-to-all-start.1 = ((bf16[8,32,1536]{2,1,0:T(8,128)(2,1)}), bf16[8,32,1536]{2,1,0:T(8,128)(2,1)S(1)}, u32[]{:S(2)}, u32[]{:S(2)}) async-start(bf16[8,32,1536]{2,1,0:T(8,128)(2,1)} %bitcast.8), calls=%async_computation.1 | async-start | bytes 1572864 | tf_op jit(solution)/shard_map/all_to_all | solution.py:44
  26.3 16.1 %all-to-all-start = ((bf16[8,32,1536]{2,1,0:T(8,128)(2,1)}), bf16[8,32,1536]{2,1,0:T(8,128)(2,1)S(1)}, u32[]{:S(2)}, u32[]{:S(2)}) async-start(bf16[8,32,1536]{2,1,0:T(8,128)(2,1)} %bitcast.3), calls=%async_computation | async-start | bytes 1572864 | tf_op jit(solution)/shard_map/all_to_all | solution.py:45
  31.3 107.6 %all-gather.9.cloned.1.call-start = ((), (), s32[]{:S(2)}) async-start(), calls=%async_computation.7 | async-start | bytes 1966080 | tf_op jit(solution)/shard_map/all_gather | solution.py:68
  49.5 198.5 %copy-start.73 = (f32[128]{0:T(128)}, f32[128]{0:T(128)S(1)}, u32[]{:S(2)}) copy-start(f32[128]{0:T(128)S(1)} %broadcast_multiply_fusion.2) | copy-start | bytes 1540
  49.7 198.3 %copy-start.79 = (f32[128]{0:T(128)}, f32[128]{0:T(128)S(1)}, u32[]{:S(2)}) copy-start(f32[128]{0:T(128)S(1)} %add_rsqrt_fusion) | copy-start | bytes 1540
  101.7 141.0 %reduce-scatter.9.cloned.1.call-start = ((), (), s32[]{:S(2)}) async-start(), calls=%async_computation.9 | async-start | bytes 3932160 | tf_op jit(solution)/shard_map/reduce_scatter | solution.py:92
  102.0 70.8 %copy-start.74 = (s32[1,512]{1,0:T(1,128)}, s32[1,512]{1,0:T(1,128)S(1)}, u32[]{:S(2)}) copy-start(s32[1,512]{1,0:T(1,128)S(1)} %broadcast_subtract_fusion) | copy-start | bytes 6148
  182.0 120.3 %reduce-scatter.11.cloned.1.call-start = ((), (), s32[]{:S(2)}) async-start(), calls=%async_computation.10 | async-start | bytes 5308416 | tf_op jit(solution)/shard_map/reduce_scatter | solution.py:103
  247.7 92.2 %all-reduce.8.cloned.1.call-start = ((), (), s32[]{:S(2)}) async-start(), calls=%async_computation.11 | async-start | bytes 393216 | tf_op jit(solution)/shard_map/psum | solution.py:130
  263.3 141.4 %reduce-scatter.7.cloned.1.call-start = ((), (), s32[]{:S(2)}) async-start(), calls=%async_computation.8 | async-start | bytes 7077888 | tf_op jit(solution)/shard_map/reduce_scatter | solution.py:89
  272.7 67.3 %copy-start.10 = (f32[1536]{0:T(1024)S(1)}, f32[1536]{0:T(1024)}, u32[]{:S(2)}) copy-start(f32[1536]{0:T(1024)} %get-tuple-element.78) | copy-start | bytes 18436
  272.7 67.3 %copy-start.11 = (f32[1536]{0:T(1024)S(1)}, f32[1536]{0:T(1024)}, u32[]{:S(2)}) copy-start(f32[1536]{0:T(1024)} %get-tuple-element.79) | copy-start | bytes 18436
  272.7 67.3 %copy-start.12 = (f32[1536]{0:T(1024)S(1)}, f32[1536]{0:T(1024)}, u32[]{:S(2)}) copy-start(f32[1536]{0:T(1024)} %get-tuple-element.80) | copy-start | bytes 18436
  272.7 67.3 %copy-start.13 = (f32[1536]{0:T(1024)S(1)}, f32[1536]{0:T(1024)}, u32[]{:S(2)}) copy-start(f32[1536]{0:T(1024)} %get-tuple-element.81) | copy-start | bytes 18436
  272.7 67.3 %copy-start.14 = (f32[1536]{0:T(1024)S(1)}, f32[1536]{0:T(1024)}, u32[]{:S(2)}) copy-start(f32[1536]{0:T(1024)} %get-tuple-element.82) | copy-start | bytes 18436
  272.7 67.3 %copy-start.15 = (f32[1536]{0:T(1024)S(1)}, f32[1536]{0:T(1024)}, u32[]{:S(2)}) copy-start(f32[1536]{0:T(1024)} %get-tuple-element.83) | copy-start | bytes 18436
  272.7 67.3 %copy-start.16 = (f32[1536]{0:T(1024)S(1)}, f32[1536]{0:T(1024)}, u32[]{:S(2)}) copy-start(f32[1536]{0:T(1024)} %get-tuple-element.84) | copy-start | bytes 18436
  272.7 67.3 %copy-start.17 = (f32[1536]{0:T(1024)S(1)}, f32[1536]{0:T(1024)}, u32[]{:S(2)}) copy-start(f32[1536]{0:T(1024)} %get-tuple-element.85) | copy-start | bytes 18436
  272.7 67.3 %copy-start.18 = (f32[1536]{0:T(1024)S(1)}, f32[1536]{0:T(1024)}, u32[]{:S(2)}) copy-start(f32[1536]{0:T(1024)} %get-tuple-element.86) | copy-start | bytes 18436
  272.8 67.3 %copy-start.19 = (f32[1536]{0:T(1024)S(1)}, f32[1536]{0:T(1024)}, u32[]{:S(2)}) copy-start(f32[1536]{0:T(1024)} %get-tuple-element.87) | copy-start | bytes 18436
  272.8 67.3 %copy-start.20 = (f32[1536]{0:T(1024)S(1)}, f32[1536]{0:T(1024)}, u32[]{:S(2)}) copy-start(f32[1536]{0:T(1024)} %get-tuple-element.88) | copy-start | bytes 18436
  272.8 67.3 %copy-start.21 = (f32[1536]{0:T(1024)S(1)}, f32[1536]{0:T(1024)}, u32[]{:S(2)}) copy-start(f32[1536]{0:T(1024)} %get-tuple-element.89) | copy-start | bytes 18436
  272.8 67.3 %copy-start.22 = (f32[1536]{0:T(1024)S(1)}, f32[1536]{0:T(1024)}, u32[]{:S(2)}) copy-start(f32[1536]{0:T(1024)} %get-tuple-element.90) | copy-start | bytes 18436
  272.8 67.3 %copy-start.23 = (f32[1536]{0:T(1024)S(1)}, f32[1536]{0:T(1024)}, u32[]{:S(2)}) copy-start(f32[1536]{0:T(1024)} %get-tuple-element.91) | copy-start | bytes 18436
  272.8 67.3 %copy-start.24 = (f32[1536]{0:T(1024)S(1)}, f32[1536]{0:T(1024)}, u32[]{:S(2)}) copy-start(f32[1536]{0:T(1024)} %get-tuple-element.92) | copy-start | bytes 18436
  272.8 67.3 %copy-start.25 = (f32[1536]{0:T(1024)S(1)}, f32[1536]{0:T(1024)}, u32[]{:S(2)}) copy-start(f32[1536]{0:T(1024)} %get-tuple-element.93) | copy-start | bytes 18436
  272.8 67.3 %copy-start.26 = (f32[1536]{0:T(1024)S(1)}, f32[1536]{0:T(1024)}, u32[]{:S(2)}) copy-start(f32[1536]{0:T(1024)} %get-tuple-element.94) | copy-start | bytes 18436
  272.8 67.3 %copy-start.27 = (f32[1536]{0:T(1024)S(1)}, f32[1536]{0:T(1024)}, u32[]{:S(2)}) copy-start(f32[1536]{0:T(1024)} %get-tuple-element.95) | copy-start | bytes 18436
  272.8 67.3 %copy-start.28 = (f32[1536]{0:T(1024)S(1)}, f32[1536]{0:T(1024)}, u32[]{:S(2)}) copy-start(f32[1536]{0:T(1024)} %get-tuple-element.96) | copy-start | bytes 18436
  272.9 67.3 %copy-start.29 = (f32[1536]{0:T(1024)S(1)}, f32[1536]{0:T(1024)}, u32[]{:S(2)}) copy-start(f32[1536]{0:T(1024)} %get-tuple-element.97) | copy-start | bytes 18436
  272.9 67.3 %copy-start.30 = (f32[1536]{0:T(1024)S(1)}, f32[1536]{0:T(1024)}, u32[]{:S(2)}) copy-start(f32[1536]{0:T(1024)} %get-tuple-element.98) | copy-start | bytes 18436
  272.9 67.3 %copy-start.31 = (f32[1536]{0:T(1024)S(1)}, f32[1536]{0:T(1024)}, u32[]{:S(2)}) copy-start(f32[1536]{0:T(1024)} %get-tuple-element.99) | copy-start | bytes 18436
  272.9 67.3 %copy-start.32 = (f32[1536]{0:T(1024)S(1)}, f32[1536]{0:T(1024)}, u32[]{:S(2)}) copy-start(f32[1536]{0:T(1024)} %get-tuple-element.100) | copy-start | bytes 18436
  272.9 67.3 %copy-start.33 = (f32[1536]{0:T(1024)S(1)}, f32[1536]{0:T(1024)}, u32[]{:S(2)}) copy-start(f32[1536]{0:T(1024)} %get-tuple-element.101) | copy-start | bytes 18436
  272.9 67.3 %copy-start.34 = (f32[1536]{0:T(1024)S(1)}, f32[1536]{0:T(1024)}, u32[]{:S(2)}) copy-start(f32[1536]{0:T(1024)} %get-tuple-element.102) | copy-start | bytes 18436
  272.9 67.3 %copy-start.35 = (f32[1536]{0:T(1024)S(1)}, f32[1536]{0:T(1024)}, u32[]{:S(2)}) copy-start(f32[1536]{0:T(1024)} %get-tuple-element.103) | copy-start | bytes 18436
  272.9 67.3 %copy-start.37 = (pred[128]{0:T(512)(128)(4,1)S(1)}, pred[128]{0:T(512)(128)(4,1)}, u32[]{:S(2)}) copy-start(pred[128]{0:T(512)(128)(4,1)} %get-tuple-element.126) | copy-start | bytes 388
  272.9 67.3 %copy-start.39 = (pred[128]{0:T(512)(128)(4,1)S(1)}, pred[128]{0:T(512)(128)(4,1)}, u32[]{:S(2)}) copy-start(pred[128]{0:T(512)(128)(4,1)} %get-tuple-element.127) | copy-start | bytes 388
  272.9 67.3 %copy-start.41 = (pred[128]{0:T(512)(128)(4,1)S(1)}, pred[128]{0:T(512)(128)(4,1)}, u32[]{:S(2)}) copy-start(pred[128]{0:T(512)(128)(4,1)} %get-tuple-element.128) | copy-start | bytes 388
  273.0 67.3 %copy-start.43 = (pred[128]{0:T(512)(128)(4,1)S(1)}, pred[128]{0:T(512)(128)(4,1)}, u32[]{:S(2)}) copy-start(pred[128]{0:T(512)(128)(4,1)} %get-tuple-element.129) | copy-start | bytes 388
  273.0 67.3 %copy-start.45 = (pred[128]{0:T(512)(128)(4,1)S(1)}, pred[128]{0:T(512)(128)(4,1)}, u32[]{:S(2)}) copy-start(pred[128]{0:T(512)(128)(4,1)} %get-tuple-element.130) | copy-start | bytes 388
  273.0 67.3 %copy-start.47 = (pred[128]{0:T(512)(128)(4,1)S(1)}, pred[128]{0:T(512)(128)(4,1)}, u32[]{:S(2)}) copy-start(pred[128]{0:T(512)(128)(4,1)} %get-tuple-element.131) | copy-start | bytes 388
  273.0 67.3 %copy-start.49 = (pred[128]{0:T(512)(128)(4,1)S(1)}, pred[128]{0:T(512)(128)(4,1)}, u32[]{:S(2)}) copy-start(pred[128]{0:T(512)(128)(4,1)} %get-tuple-element.132) | copy-start | bytes 388
  273.0 67.3 %copy-start.51 = (pred[128]{0:T(512)(128)(4,1)S(1)}, pred[128]{0:T(512)(128)(4,1)}, u32[]{:S(2)}) copy-start(pred[128]{0:T(512)(128)(4,1)} %get-tuple-element.133) | copy-start | bytes 388
  273.0 67.3 %copy-start.53 = (pred[128]{0:T(512)(128)(4,1)S(1)}, pred[128]{0:T(512)(128)(4,1)}, u32[]{:S(2)}) copy-start(pred[128]{0:T(512)(128)(4,1)} %get-tuple-element.134) | copy-start | bytes 388
  273.1 155.6 %reduce-scatter.13.cloned.1.call-start = ((), (), s32[]{:S(2)}) async-start(), calls=%async_computation.13 | async-start | bytes 983040
  304.5 181.3 %all-reduce.10.cloned.1.call-start = ((), (), s32[]{:S(2)}) async-start(), calls=%async_computation.12 | async-start | bytes 393216 | tf_op jit(solution)/shard_map/psum | solution.py:129
  (47 other events, 671.5 us)
Sparse Core Ops, SparseCore 0:
  9.6 88.0 all-gather.6
  101.9 37.0 all-gather.8
  182.1 60.5 reduce-scatter.8
  247.9 54.3 reduce-scatter.10
  305.1 34.7 all-reduce.7
  343.1 61.5 reduce-scatter.6
  407.1 21.4 reduce-scatter.12
  432.0 53.8 all-reduce.9
